TPU v7x, 256 devices: a whole 4x4x8 slice. The times are simulated.
256 devices in a mesh: dp: 2 (over z_lo), expert: 128 (over y, x, z_hi, core).
Axes of the slice: x: 4, y: 4, z: 8 (z_hi: 4, z_lo: 2; z = z_hi * 2 + z_lo), core: 2. Of those that a mesh axis runs over, the one named last changes fastest.
Arguments:
- tokens: bfloat16 [32768, 4096], P(('dp', 'expert')), may hold values from -6 to 6
- routes: int32 [256, 16, 4], P(('dp', 'expert')), may hold values from 0 to 127, as said below
- gate_values: float32 [256, 16, 4], P(('dp', 'expert')), may hold values from 0.1 to 1
- gate_weight: bfloat16 [128, 4096, 256], P('expert', 'dp'), may hold values from -0.09375 to 0.09375
- up_weight: bfloat16 [128, 4096, 256], P('expert', 'dp'), may hold values from -0.09375 to 0.09375
- down_weight: bfloat16 [128, 4096, 256], P('expert', 'dp'), may hold values from -0.125 to 0.125
- cotangent: bfloat16 [32768, 4096], P(('dp', 'expert')), may hold values from -6 to 6
Outputs:
- layer_out: bfloat16 [32768, 4096], P(('dp', 'expert'))
- token_grad: bfloat16 [32768, 4096], P(('dp', 'expert'))
- gate_grad: bfloat16 [128, 4096, 256], P('expert', 'dp')
- up_grad: bfloat16 [128, 4096, 256], P('expert', 'dp')
- down_grad: bfloat16 [128, 4096, 256], P('expert', 'dp')
Inputs may be any that keep to these rules, and one draw needn't show every extreme that they name: `routes`: for each home block and each expert, 4 distinct positions within that block.
All inputs are finite; a program needn't handle non-finite values.
Results may differ from a plain program's by a relative error of at most 0.025.
Values may be sent and summed in bfloat16 or wider, within the bound.
A program may use at most 128 MiB of HBM per device.

v0:
```python
import jax
import jax.numpy as jnp
from jax import lax
from jax.sharding import Mesh
from jax.sharding import PartitionSpec as P

SPLIT = 8
ROWS = ("dp", "yx", "col")


def send_out(payload):
    arrived = lax.all_to_all(payload, "yx", split_axis=1, concat_axis=1, tiled=True)
    shared = lax.all_gather(arrived, "col", axis=1, tiled=True)
    return shared.reshape(payload.shape[0], -1, payload.shape[-1])


def bring_back(partial_value, expert_count):
    streams, total_rows, width = partial_value.shape
    summed = lax.psum_scatter(partial_value, "col", scatter_dimension=1, tiled=True)
    summed = summed.reshape(streams, expert_count, -1, width)
    returned = lax.all_to_all(summed, "yx", split_axis=1, concat_axis=1, tiled=True)
    return returned.astype(jnp.float32)


def shards(tokens, routes, gate_values, gate_weight, up_weight, down_weight, cotangent):
    width = tokens.shape[1]
    expert_count = routes.shape[1]
    chosen = routes[0]
    scales = gate_values[0][:, :, None]
    contract_last = (((1,), (1,)), ((), ()))
    contract_first = (((0,), (0,)), ((), ()))
    weights = jnp.concatenate([gate_weight, up_weight, down_weight], axis=0)
    full = lax.all_gather(weights, "dp", axis=1, tiled=True)
    full_gate, full_up, full_down = (full[0], full[1], full[2])
    scaled_cot = (scales * cotangent[chosen].astype(jnp.float32)).astype(jnp.bfloat16)
    both_rows = send_out(jnp.stack([tokens[chosen], scaled_cot]))
    token_rows, cot_rows = (both_rows[0], both_rows[1])
    gate_pre = jnp.dot(token_rows, full_gate, preferred_element_type=jnp.float32)
    up_pre = jnp.dot(token_rows, full_up, preferred_element_type=jnp.float32)
    gate_sigma = jax.nn.sigmoid(gate_pre)
    hidden = (gate_pre * gate_sigma * up_pre).astype(jnp.bfloat16)
    partial_value = lax.dot_general(
        hidden, full_down, contract_last, preferred_element_type=jnp.float32
    ).astype(jnp.bfloat16)
    hidden_grad = jnp.dot(cot_rows, full_down, preferred_element_type=jnp.float32)
    gate_rows = (hidden_grad * up_pre * gate_sigma * (1.0 + gate_pre * (1.0 - gate_sigma))).astype(
        jnp.bfloat16
    )
    up_rows = (hidden_grad * gate_pre * gate_sigma).astype(jnp.bfloat16)
    partial_grad = (
        lax.dot_general(gate_rows, full_gate, contract_last, preferred_element_type=jnp.float32)
        + lax.dot_general(up_rows, full_up, contract_last, preferred_element_type=jnp.float32)
    ).astype(jnp.bfloat16)
    back = bring_back(jnp.stack([partial_value, partial_grad]), expert_count)
    layer_out = jnp.zeros((tokens.shape[0], width), jnp.float32).at[chosen].add(scales * back[0])
    token_grad = jnp.zeros((tokens.shape[0], width), jnp.float32).at[chosen].add(back[1])
    grad_sums = lax.psum_scatter(
        jnp.concatenate(
            [
                lax.dot_general(
                    token_rows, gate_rows, contract_first, preferred_element_type=jnp.float32
                ),
                lax.dot_general(
                    token_rows, up_rows, contract_first, preferred_element_type=jnp.float32
                ),
                lax.dot_general(
                    cot_rows, hidden, contract_first, preferred_element_type=jnp.float32
                ),
            ],
            axis=1,
        ).astype(jnp.bfloat16),
        "dp",
        scatter_dimension=0,
        tiled=True,
    ).astype(jnp.float32)
    hidden_width = hidden.shape[1]
    gate_grad = grad_sums[:, :hidden_width].astype(jnp.bfloat16)[None]
    up_grad = grad_sums[:, hidden_width : 2 * hidden_width].astype(jnp.bfloat16)[None]
    down_grad = grad_sums[:, 2 * hidden_width :].astype(jnp.bfloat16)[None]
    return (
        layer_out.astype(jnp.bfloat16),
        token_grad.astype(jnp.bfloat16),
        gate_grad,
        up_grad,
        down_grad,
    )


def solution(mesh):
    n_dp, n_expert = mesh.devices.shape
    fine = Mesh(mesh.devices.reshape(n_dp, n_expert // SPLIT, SPLIT), ROWS)
    placed = (
        P(ROWS, None),
        P(ROWS, None, None),
        P(ROWS, None, None),
        P(("yx", "col"), "dp", None),
        P(("yx", "col"), "dp", None),
        P(("yx", "col"), "dp", None),
        P(ROWS, None),
    )
    return jax.shard_map(
        shards,
        mesh=fine,
        in_specs=placed,
        out_specs=(
            P(ROWS, None),
            P(ROWS, None),
            P(("yx", "col"), "dp", None),
            P(("yx", "col"), "dp", None),
            P(("yx", "col"), "dp", None),
        ),
        check_vma=False,
    )
```

profile of v0, /device:TPU:1, one launch (start us, length us, event | category | flops | bytes accessed | tf_op | source)
XLA Modules:
  0.0 441.6 jit_solution(145172162650093640)
XLA Ops:
  11.8 23.6 %all_to_all.10 = bf16[2,16,4,4096]{3,2,0,1:T(4,128)(2,1)} all-to-all(bf16[2,16,4,4096]{3,2,0,1:T(4,128)(2,1)S(1)} %pad_maximum_fusion.3), channel_id=1, replica_groups=mesh['dp'=2,'yx'=16,'col'=8] {'yx'}, dimensions={1} | all-to-all | bytes 2097152 | tf_op jit(solution)/shard_map/all_to_all | solution.py:12
  35.5 3.7 pad_maximum_fusion.2
  39.4 75.8 %all-gather.3.cloned.1.call-done = bf16[2,128,4,4096]{3,2,0,1:T(4,128)(2,1)} async-done(((bf16[2,16,4,4096]{3,2,0,1:T(4,128)(2,1)}), bf16[2,128,4,4096]{3,2,0,1:T(4,128)(2,1)}) %all-gather.3.cloned.1.call-update) | async-done | bytes 8388624 | tf_op jit(solution)/shard_map/all_gather | solution.py:13
  115.2 10.1 %fusion.12 = (bf16[1,128,4,4096]{3,2,0,1:T(4,128)(2,1)}, bf16[1,128,4,4096]{3,2,0,1:T(4,128)(2,1)}) fusion(bf16[2,128,4,4096]{3,2,0,1:T(4,128)(2,1)} %all-gather.3.cloned.1.call-done), kind=kLoop, calls=%fused_computation.39 | loop fusion | bytes 16777216 | tf_op jit(solution)/shard_map/slice | solution.py:37
  125.3 6.9 %squeeze.25 = bf16[512,4096]{1,0:T(8,128)(2,1)} reshape(bf16[1,128,4,4096]{3,2,0,1:T(4,128)(2,1)} %get-tuple-element.26) | data formatting | bytes 8388608 | tf_op jit(solution)/shard_map/squeeze | solution.py:37
  132.3 7.1 %squeeze.29 = bf16[512,4096]{1,0:T(8,128)(2,1)} reshape(bf16[1,128,4,4096]{3,2,0,1:T(4,128)(2,1)} %get-tuple-element.25) | data formatting | bytes 8388608 | tf_op jit(solution)/shard_map/squeeze | solution.py:37
  139.4 69.8 %all-gather.5.cloned.1.call-done = bf16[3,4096,256]{2,1,0:T(8,128)(2,1)} async-done(((bf16[3,2048,256]{2,1,0:T(8,128)(2,1)}), bf16[3,4096,256]{2,1,0:T(8,128)(2,1)}) %all-gather.5.cloned.1.call-update) | async-done | bytes 6291472 | tf_op jit(solution)/shard_map/all_gather | solution.py:33
  209.2 4.2 fusion.3
  213.9 3.6 fusion.5
  217.5 1.4 multiply_convert_fusion.2
  220.2 3.3 fusion
  224.8 6.2 %pad_maximum_fusion = bf16[2,512,4096]{2,1,0:T(8,128)(2,1)} fusion(bf16[1,512,4096]{2,1,0:T(8,128)(2,1)S(1)} %fusion.1, bf16[1,512,4096]{2,1,0:T(8,128)(2,1)} %fusion), kind=kLoop, calls=%fused_computation.4 | loop fusion | flops 4194304 | bytes 16777216 | tf_op jit(solution)/shard_map/stack | solution.py:54
  231.3 3.6 convolution_convert_fusion.2
  238.5 9.5 %pad_maximum_fusion.1 = bf16[4096,768]{0,1:T(8,128)(2,1)} fusion(bf16[4096,256]{0,1:T(8,128)(2,1)S(1)} %convolution_convert_fusion.1, bf16[4096,256]{0,1:T(8,128)(2,1)S(1)} %convolution_convert_fusion.2, bf16[4096,256]{0,1:T(8,128)(2,1)S(1)} %convolution_convert_fusion.3), kind=kLoop, calls=%fused_computation.6 | loop fusion | flops 18874368 | bytes 12582912 | tf_op jit(solution)/shard_map/concatenate | solution.py:58
  248.0 79.6 %reduce-scatter.3.cloned.1.call-done = bf16[2,64,4096]{2,1,0:T(8,128)(2,1)} async-done(((bf16[2,512,4096]{2,1,0:T(8,128)(2,1)}), bf16[2,64,4096]{2,1,0:T(8,128)(2,1)}) %reduce-scatter.3.cloned.1.call-update) | async-done | bytes 1048592 | tf_op jit(solution)/shard_map/reduce_scatter | solution.py:19
  327.7 1.5 reshape.62
  329.1 1.6 copy.38
  330.7 7.1 %all-to-all-start.1 = ((bf16[2,16,4,4096]{3,2,0,1:T(4,128)(2,1)}), bf16[2,16,4,4096]{3,2,0,1:T(4,128)(2,1)S(1)}, u32[]{:S(2)}, u32[]{:S(2)}) async-start(bf16[2,16,4,4096]{3,2,0,1:T(4,128)(2,1)} %copy.38), calls=%async_computation.2 | async-start | bytes 2097152 | tf_op jit(solution)/shard_map/all_to_all | solution.py:21
  337.8 76.7 %reduce-scatter.5.cloned.1.call-done = bf16[2048,768]{0,1:T(8,128)(2,1)} async-done(((bf16[4096,768]{0,1:T(8,128)(2,1)}), bf16[2048,768]{0,1:T(8,128)(2,1)}) %reduce-scatter.5.cloned.1.call-update) | async-done | bytes 3145744 | tf_op jit(solution)/shard_map/reduce_scatter | solution.py:57
  414.5 3.2 slice_bitcast_fusion.9
  417.7 2.3 copy.39
  423.4 3.3 scatter_custom_fusion
  426.7 2.7 convert_element_type.61
  430.9 3.1 scatter_custom_fusion.1
  (50 shorter events, 17.6 us)
Async XLA Ops:
  7.2 1.2 copy-start
  7.2 2.4 copy-start.8
  7.2 2.5 copy-start.2
  7.2 108.0 %all-gather.3.cloned.1.call-start = ((), (), s32[]{:S(2)}) async-start(), calls=%async_computation.4 | async-start | bytes 9437184 | tf_op jit(solution)/shard_map/all_gather | solution.py:13
  10.8 24.7 %copy-start.7 = (bf16[1,2048,256]{2,1,0:T(8,128)(2,1)S(1)}, bf16[1,2048,256]{2,1,0:T(8,128)(2,1)}, u32[]{:S(2)}) copy-start(bf16[1,2048,256]{2,1,0:T(8,128)(2,1)} %param.12) | copy-start | bytes 3145732
  35.4 173.8 %all-gather.5.cloned.1.call-start = ((), (), s32[]{:S(2)}) async-start(), calls=%async_computation.5 | async-start | bytes 9437184 | tf_op jit(solution)/shard_map/all_gather | solution.py:33
  39.2 288.5 %reduce-scatter.3.cloned.1.call-start = ((), (), s32[]{:S(2)}) async-start(), calls=%async_computation.6 | async-start | bytes 9437184 | tf_op jit(solution)/shard_map/reduce_scatter | solution.py:19
  209.2 4.7 %copy-start.3 = (bf16[3,4096,256]{2,1,0:T(8,128)(2,1)S(1)}, bf16[3,4096,256]{2,1,0:T(8,128)(2,1)}, u32[]{:S(2)}) copy-start(bf16[3,4096,256]{2,1,0:T(8,128)(2,1)} %all-gather.5.cloned.1.call-done) | copy-start | bytes 18874372
  213.8 3.6 copy-start.4
  231.0 183.5 %reduce-scatter.5.cloned.1.call-start = ((), (), s32[]{:S(2)}) async-start(), calls=%async_computation.7 | async-start | bytes 9437184 | tf_op jit(solution)/shard_map/reduce_scatter | solution.py:57
  231.2 3.7 copy-start.5
  234.9 2.2 copy-start.6
  330.7 91.8 %all-to-all-start.1 = ((bf16[2,16,4,4096]{3,2,0,1:T(4,128)(2,1)}), bf16[2,16,4,4096]{3,2,0,1:T(4,128)(2,1)S(1)}, u32[]{:S(2)}, u32[]{:S(2)}) async-start(bf16[2,16,4,4096]{3,2,0,1:T(4,128)(2,1)} %copy.38), calls=%async_computation.2 | async-start | bytes 2097152 | tf_op jit(solution)/shard_map/all_to_all | solution.py:21
  429.4 5.7 %copy-start.1 = (bf16[128,4096]{1,0:T(8,128)(2,1)S(1)}, bf16[128,4096]{1,0:T(8,128)(2,1)}, u32[]{:S(2)}) copy-start(bf16[128,4096]{1,0:T(8,128)(2,1)} %param.13) | copy-start | bytes 3145732
Sparse Core Ops, SparseCore 0:
  35.5 79.6 all-gather.2
  117.0 92.1 all-gather.4
  231.1 96.5 reduce-scatter.2
  330.1 84.3 reduce-scatter.4
where the time goes:
time: 442 us
  waiting for transfers between devices  302 us (68%)
  local copies, waits for them, and re-layouts  40.9 us (9%)
  other arithmetic  31.9 us (7%)
  blocking collectives  23.6 us (5%)
  matrix products  21.5 us (5%)
  between operations  14 us (3%)
  starting transfers between devices  7.63 us (2%)
    reduce_scatter x1, waiting for transfers between devices, bring_back(): lax.psum_scatter(partial_value, 'col', scatter_dimension=1, tiled=True)  79.6 us
    reduce_scatter x1, waiting for transfers between devices, shards(): lax.psum_scatter(jnp.concatenate([lax.dot_general(token_rows, gate_rows,...  76.7 us
    all_gather x1, waiting for transfers between devices, send_out(): shared = lax.all_gather(arrived, 'col', axis=1, tiled=True)  75.8 us
    all_gather x1, waiting for transfers between devices, shards(): full = lax.all_gather(weights, 'dp', axis=1, tiled=True)  69.8 us
    all_to_all x1, blocking collectives, send_out(): lax.all_to_all(payload, 'yx', split_axis=1, concat_axis=1, tiled=True)  23.6 us
    squeeze x2, local copies, waits for them, and re-layouts, shards(): token_rows, cot_rows = (both_rows[0], both_rows[1])  14 us
    slice x1, local copies, waits for them, and re-layouts, shards(): token_rows, cot_rows = (both_rows[0], both_rows[1])  10.1 us
    concatenate x1, other arithmetic, shards(): jnp.concatenate([lax.dot_general(token_rows, gate_rows, contract_first, p...  9.54 us
  transfers between devices with their start and end apart: 5, of which 4 were waited for; matrix products, arithmetic and copies ran while one was open for 12% of the time, Pallas kernels for 0%

commit v1 on v0

--- a/solution.py
+++ b/solution.py
@@ -10,7 +10,8 @@
 
 def send_out(payload):
     arrived = lax.all_to_all(payload, "yx", split_axis=1, concat_axis=1, tiled=True)
-    shared = lax.all_gather(arrived, "col", axis=1, tiled=True)
+    outgoing = jnp.stack([arrived] * lax.axis_size("col"))
+    shared = jnp.concatenate(lax.all_to_all(outgoing, "col", 0, 0), axis=1)
     return shared.reshape(payload.shape[0], -1, payload.shape[-1])
 
 

time: 442 us -> 557 us (1.26)
  waiting for transfers between devices: 302 us -> 400 us
  starting transfers between devices: 7.63 us -> 18.4 us
  local copies, waits for them, and re-layouts: 40.9 us -> 48.6 us
    all_to_all x0 -> x1, waiting for transfers between devices: none -> 245 us  [send_out(): shared = jnp.concatenate(lax.all_to_all(outgoing, 'col', 0, 0), axis=1)]
    all_gather x1 -> x0, waiting for transfers between devices: 75.8 us -> none  [send_out(): shared = lax.all_gather(arrived, 'col', axis=1, tiled=True)]
    all_gather x1, waiting for transfers between devices: 69.8 us -> 0.01 us  [shards(): full = lax.all_gather(weights, 'dp', axis=1, tiled=True)]
    all_to_all x0 -> x1, starting transfers between devices: none -> 10.7 us  [send_out(): shared = jnp.concatenate(lax.all_to_all(outgoing, 'col', 0, 0), axis=1)]
    another operation x0 -> x1, local copies, waits for them, and re-layouts: none -> 7.5 us  [send_out(): outgoing = jnp.stack([arrived] * lax.axis_size('col'))]
  transfers between devices with their start and end apart: 5 -> 5, of which waited for: 4 -> 3; matrix products, arithmetic and copies ran while one was open for 12% -> 10% of each run, Pallas kernels for 0% -> 0%
where the time goes in v1:
time: 557 us; the launch traced here: 556 us
  waiting for transfers between devices  400 us (72%)
  local copies, waits for them, and re-layouts  48.6 us (9%)
  other arithmetic  30.4 us (5%)
  blocking collectives  23.5 us (4%)
  matrix products  21.5 us (4%)
  starting transfers between devices  18.4 us (3%)
  between operations  14 us (3%)
    all_to_all x1, waiting for transfers between devices, send_out(): shared = jnp.concatenate(lax.all_to_all(outgoing, 'col', 0, 0), axis=1)  245 us
    reduce_scatter x1, waiting for transfers between devices, bring_back(): lax.psum_scatter(partial_value, 'col', scatter_dimension=1, tiled=True)  77.6 us
    reduce_scatter x1, waiting for transfers between devices, shards(): lax.psum_scatter(jnp.concatenate([lax.dot_general(token_rows, gate_rows,...  77.4 us
    all_to_all x1, blocking collectives, send_out(): lax.all_to_all(payload, 'yx', split_axis=1, concat_axis=1, tiled=True)  23.5 us
    squeeze x2, local copies, waits for them, and re-layouts, shards(): token_rows, cot_rows = (both_rows[0], both_rows[1])  13.8 us
  transfers between devices with their start and end apart: 5, of which 3 were waited for; matrix products, arithmetic and copies ran while one was open for 10% of the time, Pallas kernels for 0%

profile of v1, /device:TPU:1, one launch (start us, length us, event | category | flops | bytes accessed | tf_op | source)
XLA Modules:
  0.0 556.5 jit_solution(17178390444024709563)
XLA Ops:
  11.8 23.5 %all_to_all.15 = bf16[2,16,4,4096]{3,2,0,1:T(4,128)(2,1)S(1)} all-to-all(bf16[2,16,4,4096]{3,2,0,1:T(4,128)(2,1)S(1)} %pad_maximum_fusion.3), channel_id=1, replica_groups=mesh['dp'=2,'yx'=16,'col'=8] {'yx'}, dimensions={1} | all-to-all | bytes 2097152 | tf_op jit(solution)/shard_map/all_to_all | solution.py:12
  35.7 7.5 %stack.14 = bf16[8,2,16,4,4096]{4,3,2,1,0:T(4,128)(2,1)} broadcast(bf16[2,16,4,4096]{3,2,1,0:T(4,128)(2,1)S(1)} %copy.29), dimensions={1,2,3,4} | broadcast | bytes 9437184 | tf_op jit(solution)/shard_map/stack | solution.py:13
  43.2 10.7 %all-to-all-start.1 = ((bf16[8,2,16,4,4096]{4,3,2,1,0:T(4,128)(2,1)}), bf16[8,2,16,4,4096]{4,3,2,1,0:T(4,128)(2,1)}, u32[]{:S(2)}, u32[]{:S(2)}) async-start(bf16[8,2,16,4,4096]{4,3,2,1,0:T(4,128)(2,1)} %stack.14), calls=%async_computation.1 | async-start | bytes 16777216 | tf_op jit(solution)/shard_map/all_to_all | solution.py:14
  53.9 2.1 pad_maximum_fusion.2
  56.3 245.2 %all-to-all-done.1 = bf16[8,2,16,4,4096]{4,3,2,1,0:T(4,128)(2,1)} async-done(((bf16[8,2,16,4,4096]{4,3,2,1,0:T(4,128)(2,1)}), bf16[8,2,16,4,4096]{4,3,2,1,0:T(4,128)(2,1)}, u32[]{:S(2)}, u32[]{:S(2)}) %all-to-all-start.1) | async-done | bytes 8388640 | tf_op jit(solution)/shard_map/all_to_all | solution.py:14
  301.5 10.0 %fusion.12 = (bf16[1,8,16,4,4096]{4,3,2,0,1:T(4,128)(2,1)}, bf16[1,8,16,4,4096]{4,3,2,0,1:T(4,128)(2,1)}) fusion(bf16[2,8,16,4,4096]{4,3,2,0,1:T(4,128)(2,1)} %bitcast.4), kind=kLoop, calls=%fused_computation.39 | loop fusion | bytes 16777216 | tf_op jit(solution)/shard_map/slice | solution.py:38
  311.5 6.9 %squeeze.25 = bf16[512,4096]{1,0:T(8,128)(2,1)} reshape(bf16[1,8,16,4,4096]{4,3,2,0,1:T(4,128)(2,1)} %get-tuple-element.21) | data formatting | bytes 8388608 | tf_op jit(solution)/shard_map/squeeze | solution.py:38
  318.4 6.9 %squeeze.29 = bf16[512,4096]{1,0:T(8,128)(2,1)} reshape(bf16[1,8,16,4,4096]{4,3,2,0,1:T(4,128)(2,1)} %get-tuple-element.20) | data formatting | bytes 8388608 | tf_op jit(solution)/shard_map/squeeze | solution.py:38
  325.3 4.2 fusion.3
  330.0 3.6 fusion.5
  336.3 3.2 fusion
  340.9 6.2 %pad_maximum_fusion = bf16[2,512,4096]{2,1,0:T(8,128)(2,1)} fusion(bf16[1,512,4096]{2,1,0:T(8,128)(2,1)S(1)} %fusion.1, bf16[1,512,4096]{2,1,0:T(8,128)(2,1)} %fusion), kind=kLoop, calls=%fused_computation.4 | loop fusion | flops 4194304 | bytes 16777216 | tf_op jit(solution)/shard_map/stack | solution.py:55
  347.4 3.6 convolution_convert_fusion.2
  354.6 9.6 %pad_maximum_fusion.1 = bf16[4096,768]{0,1:T(8,128)(2,1)} fusion(bf16[4096,256]{0,1:T(8,128)(2,1)S(1)} %convolution_convert_fusion.1, bf16[4096,256]{0,1:T(8,128)(2,1)S(1)} %convolution_convert_fusion.2, bf16[4096,256]{0,1:T(8,128)(2,1)S(1)} %convolution_convert_fusion.3), kind=kLoop, calls=%fused_computation.6 | loop fusion | flops 18874368 | bytes 12582912 | tf_op jit(solution)/shard_map/concatenate | solution.py:59
  364.1 77.6 %reduce-scatter.3.cloned.1.call-done = bf16[2,64,4096]{2,1,0:T(8,128)(2,1)} async-done(((bf16[2,512,4096]{2,1,0:T(8,128)(2,1)}), bf16[2,64,4096]{2,1,0:T(8,128)(2,1)}) %reduce-scatter.3.cloned.1.call-update) | async-done | bytes 1048592 | tf_op jit(solution)/shard_map/reduce_scatter | solution.py:20
  441.7 1.5 reshape.67
  443.2 1.6 copy.30
  444.8 7.2 %all-to-all-start.2 = ((bf16[2,16,4,4096]{3,2,0,1:T(4,128)(2,1)}), bf16[2,16,4,4096]{3,2,0,1:T(4,128)(2,1)S(1)}, u32[]{:S(2)}, u32[]{:S(2)}) async-start(bf16[2,16,4,4096]{3,2,0,1:T(4,128)(2,1)} %copy.30), calls=%async_computation.3 | async-start | bytes 2097152 | tf_op jit(solution)/shard_map/all_to_all | solution.py:22
  452.0 77.4 %reduce-scatter.5.cloned.1.call-done = bf16[2048,768]{0,1:T(8,128)(2,1)} async-done(((bf16[4096,768]{0,1:T(8,128)(2,1)}), bf16[2048,768]{0,1:T(8,128)(2,1)}) %reduce-scatter.5.cloned.1.call-update) | async-done | bytes 3145744 | tf_op jit(solution)/shard_map/reduce_scatter | solution.py:58
  529.4 3.2 slice_bitcast_fusion.9
  532.5 2.3 copy.31
  538.3 3.3 scatter_custom_fusion
  541.6 2.7 convert_element_type.61
  545.8 3.1 scatter_custom_fusion.1
  (55 shorter events, 19.4 us)
Async XLA Ops:
  7.2 1.2 copy-start
  7.2 2.4 copy-start.10
  7.2 2.5 copy-start.2
  43.2 10.7 %copy-start.7 = (bf16[1,2048,256]{2,1,0:T(8,128)(2,1)S(1)}, bf16[1,2048,256]{2,1,0:T(8,128)(2,1)}, u32[]{:S(2)}) copy-start(bf16[1,2048,256]{2,1,0:T(8,128)(2,1)} %param.12) | copy-start | bytes 3145732
  43.2 10.7 %copy-start.8 = (bf16[1,2048,256]{2,1,0:T(8,128)(2,1)S(1)}, bf16[1,2048,256]{2,1,0:T(8,128)(2,1)}, u32[]{:S(2)}) copy-start(bf16[1,2048,256]{2,1,0:T(8,128)(2,1)} %param.11) | copy-start | bytes 3145732
  43.2 10.7 %copy-start.9 = (bf16[1,2048,256]{2,1,0:T(8,128)(2,1)S(1)}, bf16[1,2048,256]{2,1,0:T(8,128)(2,1)}, u32[]{:S(2)}) copy-start(bf16[1,2048,256]{2,1,0:T(8,128)(2,1)} %param.10) | copy-start | bytes 3145732
  43.2 258.3 %all-to-all-start.1 = ((bf16[8,2,16,4,4096]{4,3,2,1,0:T(4,128)(2,1)}), bf16[8,2,16,4,4096]{4,3,2,1,0:T(4,128)(2,1)}, u32[]{:S(2)}, u32[]{:S(2)}) async-start(bf16[8,2,16,4,4096]{4,3,2,1,0:T(4,128)(2,1)} %stack.14), calls=%async_computation.1 | async-start | bytes 16777216 | tf_op jit(solution)/shard_map/all_to_all | solution.py:14
  53.9 271.4 %all-gather.2.cloned.1.call-start = ((), (), s32[]{:S(2)}) async-start(), calls=%async_computation.5 | async-start | bytes 9437184 | tf_op jit(solution)/shard_map/all_gather | solution.py:34
  56.1 385.6 %reduce-scatter.3.cloned.1.call-start = ((), (), s32[]{:S(2)}) async-start(), calls=%async_computation.6 | async-start | bytes 9437184 | tf_op jit(solution)/shard_map/reduce_scatter | solution.py:20
  325.3 4.7 copy-start.3
  330.0 3.6 copy-start.4
  347.1 182.3 %reduce-scatter.5.cloned.1.call-start = ((), (), s32[]{:S(2)}) async-start(), calls=%async_computation.7 | async-start | bytes 9437184 | tf_op jit(solution)/shard_map/reduce_scatter | solution.py:58
  347.4 3.7 copy-start.5
  351.0 2.2 copy-start.6
  444.8 92.6 %all-to-all-start.2 = ((bf16[2,16,4,4096]{3,2,0,1:T(4,128)(2,1)}), bf16[2,16,4,4096]{3,2,0,1:T(4,128)(2,1)S(1)}, u32[]{:S(2)}, u32[]{:S(2)}) async-start(bf16[2,16,4,4096]{3,2,0,1:T(4,128)(2,1)} %copy.30), calls=%async_computation.3 | async-start | bytes 2097152 | tf_op jit(solution)/shard_map/all_to_all | solution.py:22
  544.3 5.7 %copy-start.1 = (bf16[128,4096]{1,0:T(8,128)(2,1)S(1)}, bf16[128,4096]{1,0:T(8,128)(2,1)}, u32[]{:S(2)}) copy-start(bf16[128,4096]{1,0:T(8,128)(2,1)} %param.13) | copy-start | bytes 3145732
Sparse Core Ops, SparseCore 0:
  56.5 219.7 all-gather.1
  347.2 94.4 reduce-scatter.2
  444.3 85.0 reduce-scatter.4
